TPU v7x, 256 devices: a whole 4x4x8 slice. The times are simulated.
256 devices in a mesh: slab: 8 (over z), front: 32 (over y, x, core).
Axes of the slice: x: 4, y: 4, z: 8, core: 2. Of those that a mesh axis runs over, the one named last changes fastest.
Arguments:
- leaf_rhs: bfloat16 [8, 2, 512, 128, 512], P('slab', None, 'front'), may hold values from -6 to 6
- leaf_inv: bfloat16 [8, 512, 2, 128, 128], P('slab', 'front'), may hold values from -0.375 to 0.375
- leaf_off: bfloat16 [8, 512, 2, 128, 128], P('slab', 'front'), may hold values from -0.125 to 0.125
- parent: int32 [8, 512, 1], P('slab', 'front'), may hold values from 0 to 31; in each aligned block of 16 rows (0 to 15, 16 to 31, ..., all dimensions but the last counted through in order) no two rows name the same one
- ancestors: int32 [8, 512, 128], P('slab', 'front'), may hold values from 0 to 255
- root_rhs: bfloat16 [8, 2, 8192, 512], P('slab', None, 'front'), may hold values from -6 to 6
- root_inv: float32 [8, 64, 2, 128, 128], P('slab', 'front'), may hold values from -2 to 2.5
- coupling: float32 [8, 8192], P('slab', 'front'), may hold values from 0.6 to 1.3
Outputs:
- leaf_sol: bfloat16 [8, 2, 512, 128, 512], P('slab', None, 'front')
- root_sol: float32 [8, 2, 8192, 512], P('slab', None, 'front')
Inputs may be any that keep to these rules, and one draw needn't show every extreme that they name: Each front index's 16 leaf blocks of a slab name any one parent at most 1 times. `ancestors`: rows may repeat within a block.
All inputs are finite; a program needn't handle non-finite values.
Results may differ from a plain program's by a relative error of at most 0.0057.
Values may be sent and summed in bfloat16 or wider, within the bound.
A program may use at most 128 MiB of HBM per device.

v0:
```python
import jax
import jax.numpy as jnp
from jax import lax
from jax.sharding import PartitionSpec as P


def passed_along(x, axis, by):
    count = lax.axis_size(axis)
    pairs = [(i, i + by) for i in range(count) if 0 <= i + by < count]
    return lax.ppermute(x, axis, pairs)


def planes_apply(real_mat, imag_mat, real_vec, imag_vec, form):
    real = jnp.einsum(form, real_mat, real_vec, preferred_element_type=jnp.float32) - jnp.einsum(
        form, imag_mat, imag_vec, preferred_element_type=jnp.float32
    )
    imag = jnp.einsum(form, real_mat, imag_vec, preferred_element_type=jnp.float32) + jnp.einsum(
        form, imag_mat, real_vec, preferred_element_type=jnp.float32
    )
    return jnp.stack([real, imag])


def block_solve(blocks, field):
    highest = lax.Precision.HIGHEST
    shaped = field.reshape(2, blocks.shape[0], blocks.shape[2], field.shape[-1])
    real = jnp.einsum("kij,kjc->kic", blocks[:, 0], shaped[0], precision=highest) - jnp.einsum(
        "kij,kjc->kic", blocks[:, 1], shaped[1], precision=highest
    )
    imag = jnp.einsum("kij,kjc->kic", blocks[:, 0], shaped[1], precision=highest) + jnp.einsum(
        "kij,kjc->kic", blocks[:, 1], shaped[0], precision=highest
    )
    return jnp.stack([real, imag]).reshape(field.shape)


def body(leaf_rhs, leaf_inv, leaf_off, parent, ancestors, root_rhs, root_inv, coupling):
    forward_form = "lij,ljc->lic"
    back_form = "lji,ljc->lic"
    rhs = leaf_rhs[0]
    inverse = leaf_inv[0]
    offdiag = leaf_off[0]
    owners = parent[0, :, 0]
    anc_rows = ancestors[0]
    fronts = lax.axis_size("front")
    count = owners.shape[0]
    per_owner = (count + fronts - 1) // fronts
    blk = rhs.shape[2]
    width = rhs.shape[3]
    root_rows = root_rhs.shape[2]
    slot_total = fronts * per_owner
    hits = (owners[:, None] == jnp.arange(fronts, dtype=jnp.int32)[None, :]).astype(jnp.int32)
    rank = jnp.sum((jnp.cumsum(hits, axis=0) - hits) * hits, axis=1)
    slot = owners * per_owner + rank
    place_int = (slot[:, None] == jnp.arange(slot_total, dtype=jnp.int32)[None, :]).astype(
        jnp.int32
    )
    place = place_int.astype(jnp.bfloat16)
    slot_ids = jnp.sum(place_int[:, :, None] * anc_rows[:, None, :], axis=0).reshape(
        1, fronts, per_owner, blk
    )
    forward = planes_apply(inverse[:, 0], inverse[:, 1], rhs[0], rhs[1], forward_form).astype(
        jnp.bfloat16
    )
    partial_value = planes_apply(
        offdiag[:, 0], offdiag[:, 1], forward[0], forward[1], forward_form
    ).astype(jnp.bfloat16)
    placed = jnp.einsum(
        "ks,pkbc->psbc", place, partial_value, preferred_element_type=jnp.float32
    ).astype(jnp.bfloat16)
    placed = placed.reshape(2, fronts, per_owner, blk, width)
    arrived, arrived_ids = (
        lax.all_to_all(placed, "front", split_axis=1, concat_axis=1, tiled=True),
        lax.all_to_all(slot_ids, "front", split_axis=1, concat_axis=1, tiled=True),
    )
    slot_parts = arrived.reshape(2, slot_total * blk, width)
    flat_ids = arrived_ids.reshape(-1)
    row_table = (flat_ids[:, None] == jnp.arange(root_rows, dtype=jnp.int32)[None, :]).astype(
        jnp.bfloat16
    )
    summed = jnp.einsum("sr,psc->prc", row_table, slot_parts, preferred_element_type=jnp.float32)
    reduced = root_rhs[0].astype(jnp.float32) - summed
    blocks = root_inv[0]
    cpl = coupling[0]
    first = block_solve(blocks, reduced)

    def relay(step, state):
        previous = passed_along(state, "slab", 1)
        return block_solve(blocks, reduced - cpl[None, :, None] * previous)

    state = lax.fori_loop(0, lax.axis_size("slab") - 1, relay, first)
    root_half = state.astype(jnp.bfloat16)
    slot_rows = jnp.einsum(
        "sr,prc->psc", row_table, root_half, preferred_element_type=jnp.float32
    ).astype(jnp.bfloat16)
    slot_rows = slot_rows.reshape(2, fronts, per_owner, blk, width)
    returned = lax.all_to_all(slot_rows, "front", split_axis=1, concat_axis=1, tiled=True)
    picked = jnp.einsum(
        "ks,psbc->pkbc",
        place,
        returned.reshape(2, slot_total, blk, width),
        preferred_element_type=jnp.float32,
    ).astype(jnp.bfloat16)
    back = planes_apply(offdiag[:, 0], offdiag[:, 1], picked[0], picked[1], back_form).astype(
        jnp.bfloat16
    )
    solved = forward.astype(jnp.float32) - planes_apply(
        inverse[:, 0], inverse[:, 1], back[0], back[1], forward_form
    )
    return (solved.astype(jnp.bfloat16)[None], state[None])


def solution(mesh):
    in_specs = (
        P("slab", None, "front", None, None),
        P("slab", "front", None, None, None),
        P("slab", "front", None, None, None),
        P("slab", "front", None),
        P("slab", "front", None),
        P("slab", None, "front", None),
        P("slab", "front", None, None, None),
        P("slab", "front"),
    )
    out_specs = (P("slab", None, "front", None, None), P("slab", None, "front", None))
    return jax.shard_map(body, mesh=mesh, in_specs=in_specs, out_specs=out_specs, check_vma=False)
```

profile of v0, /device:TPU:129, one launch (start us, length us, event | category | flops | bytes accessed | tf_op | source)
XLA Modules:
  0.0 566.3 jit_solution(2342361114886660467)
XLA Ops:
  2.1 4.8 fusion.20
  6.9 2.7 fusion.24
  10.0 3.9 add_convert_fusion.2
  19.8 2.4 pad_maximum_fusion.1
  22.2 8.3 %copy.77 = bf16[2,16,128,512]{3,1,2,0:T(8,128)(2,1)} copy(bf16[2,16,128,512]{2,3,1,0:T(8,128)(2,1)} %pad_maximum_fusion.1) | data formatting | bytes 8388608 | tf_op jit(solution)/shard_map/stack | solution.py:20
  30.6 7.9 %convert_bitcast_fusion = bf16[2,32,1,128,512]{4,1,3,0,2:T(8,128)(2,1)} fusion(bf16[2,16,128,512]{3,1,2,0:T(8,128)(2,1)} %copy.77, s32[16]{0:T(128)S(1)} %bitcast_add_fusion), kind=kOutput, calls=%fused_computation.19 | convolution fusion | flops 138413568 | bytes 12582976 | tf_op jit(solution)/shard_map/ks,pkbc->psbc/dot_general | solution.py:66
  38.4 11.4 %copy.78 = bf16[2,32,1,128,512]{4,3,0,2,1:T(8,128)(2,1)} copy(bf16[2,32,1,128,512]{4,1,3,0,2:T(8,128)(2,1)} %convert_bitcast_fusion) | data formatting | bytes 16777216 | tf_op jit(solution)/shard_map/reshape | solution.py:69
  49.8 8.0 %all-to-all-start = ((bf16[2,32,1,128,512]{4,3,0,2,1:T(8,128)(2,1)}), bf16[2,32,1,128,512]{4,3,0,2,1:T(8,128)(2,1)}, u32[]{:S(2)}, u32[]{:S(2)}) async-start(bf16[2,32,1,128,512]{4,3,0,2,1:T(8,128)(2,1)} %copy.78), calls=%async_computation | async-start | bytes 16777216 | tf_op jit(solution)/shard_map/all_to_all | solution.py:71
  58.6 99.9 %all-to-all-done = bf16[2,32,1,128,512]{4,3,0,2,1:T(8,128)(2,1)} async-done(((bf16[2,32,1,128,512]{4,3,0,2,1:T(8,128)(2,1)}), bf16[2,32,1,128,512]{4,3,0,2,1:T(8,128)(2,1)}, u32[]{:S(2)}, u32[]{:S(2)}) %all-to-all-start) | async-done | bytes 8388640 | tf_op jit(solution)/shard_map/all_to_all | solution.py:71
  158.4 9.2 %all-to-all-start.1 = ((s32[1,32,1,128]{3,2,0,1:T(1,128)}), s32[1,32,1,128]{3,2,0,1:T(1,128)S(1)}, u32[]{:S(2)}, u32[]{:S(2)}) async-start(s32[1,32,1,128]{3,2,0,1:T(1,128)} %bitcast.32), calls=%async_computation.1 | async-start | bytes 32768 | tf_op jit(solution)/shard_map/all_to_all | solution.py:72
  167.7 7.6 %copy.79 = bf16[2,32,1,128,512]{4,3,1,0,2:T(8,128)(2,1)} copy(bf16[2,32,1,128,512]{4,3,0,2,1:T(8,128)(2,1)} %all-to-all-done) | data formatting | bytes 16777216 | tf_op jit(solution)/shard_map/all_to_all | solution.py:71
  175.3 6.7 %fusion.37 = f32[2,256,512]{2,1,0:T(8,128)S(1)} fusion(bf16[2,4096,512]{2,1,0:T(8,128)(2,1)} %bitcast.229, s32[4096]{0:T(1024)S(1)} %bitcast.237, bf16[1,2,256,512]{3,2,1,0:T(8,128)(2,1)} %param.15), kind=kOutput, calls=%fused_computation.51 | convolution fusion | flops 2149056512 | bytes 9977856 | tf_op jit(solution)/shard_map/sr,psc->prc/dot_general | solution.py:79
  185.6 212.0 %while.10 = (s32[]{:T(128)}, f32[2,256,512]{2,1,0:T(8,128)}, f32[1,256]{1,0:T(1,128)S(1)}, f32[2,256,512]{2,1,0:T(8,128)S(1)}, f32[2,2,128,128]{3,2,0,1:T(8,128)S(1)}, /*index=5*/s32[]{:T(128)}) while((s32[]{:T(128)}, f32[2,256,512]{2,1,0:T(8,128)}, f32[1,256]{1,0:T(1,128)S(1)}, f32[2,256,512]{2,1,0:T(8,128)S(1)}, ...), condition=%wide.region_4.5_spmd, body=%wide.region_3.4_spmd.sunk | while | flops 806354944 | bytes 17302636 | solution.py:89
  185.6 2.6 collective-permute-start
  188.2 25.3 %collective-permute-done = f32[2,256,512]{2,1,0:T(8,128)} collective-permute-done((f32[2,256,512]{2,1,0:T(8,128)}, f32[2,256,512]{2,1,0:T(8,128)}, u32[]{:S(2)}, u32[]{:S(2)}) %collective-permute-start) | collective-permute-done | bytes 1048608 | tf_op jit(solution)/shard_map/while/body/eval_jaxpr/ppermute | solution.py:10
  218.4 1.9 collective-permute-start
  220.4 25.1 %collective-permute-done = f32[2,256,512]{2,1,0:T(8,128)} collective-permute-done((f32[2,256,512]{2,1,0:T(8,128)}, f32[2,256,512]{2,1,0:T(8,128)}, u32[]{:S(2)}, u32[]{:S(2)}) %collective-permute-start) | collective-permute-done | bytes 1048608 | tf_op jit(solution)/shard_map/while/body/eval_jaxpr/ppermute | solution.py:10
  252.4 24.3 %collective-permute-done = f32[2,256,512]{2,1,0:T(8,128)} collective-permute-done((f32[2,256,512]{2,1,0:T(8,128)}, f32[2,256,512]{2,1,0:T(8,128)}, u32[]{:S(2)}, u32[]{:S(2)}) %collective-permute-start) | collective-permute-done | bytes 1048608 | tf_op jit(solution)/shard_map/while/body/eval_jaxpr/ppermute | solution.py:10
  283.5 23.4 %collective-permute-done = f32[2,256,512]{2,1,0:T(8,128)} collective-permute-done((f32[2,256,512]{2,1,0:T(8,128)}, f32[2,256,512]{2,1,0:T(8,128)}, u32[]{:S(2)}, u32[]{:S(2)}) %collective-permute-start) | collective-permute-done | bytes 1048608 | tf_op jit(solution)/shard_map/while/body/eval_jaxpr/ppermute | solution.py:10
  313.8 22.6 %collective-permute-done = f32[2,256,512]{2,1,0:T(8,128)} collective-permute-done((f32[2,256,512]{2,1,0:T(8,128)}, f32[2,256,512]{2,1,0:T(8,128)}, u32[]{:S(2)}, u32[]{:S(2)}) %collective-permute-start) | collective-permute-done | bytes 1048608 | tf_op jit(solution)/shard_map/while/body/eval_jaxpr/ppermute | solution.py:10
  343.2 21.7 %collective-permute-done = f32[2,256,512]{2,1,0:T(8,128)} collective-permute-done((f32[2,256,512]{2,1,0:T(8,128)}, f32[2,256,512]{2,1,0:T(8,128)}, u32[]{:S(2)}, u32[]{:S(2)}) %collective-permute-start) | collective-permute-done | bytes 1048608 | tf_op jit(solution)/shard_map/while/body/eval_jaxpr/ppermute | solution.py:10
  371.8 20.8 %collective-permute-done = f32[2,256,512]{2,1,0:T(8,128)} collective-permute-done((f32[2,256,512]{2,1,0:T(8,128)}, f32[2,256,512]{2,1,0:T(8,128)}, u32[]{:S(2)}, u32[]{:S(2)}) %collective-permute-start) | collective-permute-done | bytes 1048608 | tf_op jit(solution)/shard_map/while/body/eval_jaxpr/ppermute | solution.py:10
  397.6 6.7 %convolution_convert_fusion = bf16[2,512,4096]{2,1,0:T(8,128)(2,1)} fusion(s32[4096]{0:T(1024)S(1)} %bitcast.238, f32[2,256,512]{2,1,0:T(8,128)} %get-tuple-element.29), kind=kOutput, calls=%fused_computation.20 | convolution fusion | flops 2152988672 | bytes 9453568 | tf_op jit(solution)/shard_map/sr,prc->psc/dot_general | solution.py:91
  404.3 9.4 %copy.106 = bf16[128,8,32,128]{3,2,1,0:T(8,128)(2,1)} copy(bf16[128,8,32,128]{3,1,2,0:T(8,128)(2,1)} %bitcast.209) | data formatting | bytes 16777216
  413.7 14.0 %copy.84 = bf16[2,32,1,128,512]{4,3,0,2,1:T(8,128)(2,1)} copy(bf16[2,32,1,128,512]{3,1,4,0,2:T(8,128)(2,1)} %bitcast.210) | data formatting | bytes 16777216 | tf_op jit(solution)/shard_map/reshape | solution.py:94
  427.7 108.1 %all_to_all.15 = bf16[2,32,1,128,512]{4,3,0,2,1:T(8,128)(2,1)S(1)} all-to-all(bf16[2,32,1,128,512]{4,3,0,2,1:T(8,128)(2,1)} %copy.84), channel_id=1, replica_groups=mesh['slab'=8,'front'=32] {'front'}, dimensions={1} | all-to-all | bytes 16777216 | tf_op jit(solution)/shard_map/all_to_all | solution.py:95
  535.8 5.9 %convert_bitcast_fusion.1 = bf16[2,16,128,512]{3,1,2,0:T(8,128)(2,1)S(1)} fusion(bf16[2,32,1,128,512]{4,3,0,2,1:T(8,128)(2,1)S(1)} %all_to_all.15, s32[16]{0:T(128)S(1)} %bitcast_add_fusion), kind=kOutput, calls=%fused_computation.26 | convolution fusion | flops 136316416 | bytes 12582976 | tf_op jit(solution)/shard_map/ks,psbc->pkbc/dot_general | solution.py:96
  541.7 2.5 slice_bitcast_fusion.1
  544.2 4.7 copy.86
  548.8 4.5 copy.87
  553.3 2.4 fusion.43
  563.1 3.0 fusion.10
  (114 shorter events, 63.3 us)
Async XLA Ops:
  0.6 6.3 %copy-start.8 = (bf16[1,2,16,128,512]{4,3,2,1,0:T(8,128)(2,1)S(1)}, bf16[1,2,16,128,512]{4,3,2,1,0:T(8,128)(2,1)}, u32[]{:S(2)}) copy-start(bf16[1,2,16,128,512]{4,3,2,1,0:T(8,128)(2,1)} %param.10) | copy-start | bytes 12582916
  2.1 11.8 %copy-start.4 = (bf16[1,16,2,128,128]{4,3,1,2,0:T(8,128)(2,1)}, bf16[1,16,2,128,128]{4,3,1,2,0:T(8,128)(2,1)S(1)}, u32[]{:S(2)}) copy-start(bf16[1,16,2,128,128]{4,3,1,2,0:T(8,128)(2,1)S(1)} %copy.117) | copy-start | bytes 3145732
  6.9 2.7 copy-start.15
  6.9 3.0 copy-start.11
  10.0 8.9 %copy-start.2 = (bf16[1,16,2,128,128]{4,3,1,2,0:T(8,128)(2,1)}, bf16[1,16,2,128,128]{4,3,1,2,0:T(8,128)(2,1)S(1)}, u32[]{:S(2)}) copy-start(bf16[1,16,2,128,128]{4,3,1,2,0:T(8,128)(2,1)S(1)} %copy.116) | copy-start | bytes 3145732
  10.0 4.4 copy-start.9
  10.0 5.7 copy-start.10
  16.4 1.6 copy-start
  49.8 8.0 %copy-start.14 = (s32[1,16,128]{2,1,0:T(8,128)S(1)}, s32[1,16,128]{2,1,0:T(8,128)}, u32[]{:S(2)}) copy-start(s32[1,16,128]{2,1,0:T(8,128)} %param.14) | copy-start | bytes 24580
  49.8 117.9 %copy-start.12 = (f32[1,2,2,128,128]{4,3,2,1,0:T(8,128)S(1)}, f32[1,2,2,128,128]{4,3,2,1,0:T(8,128)}, u32[]{:S(2)}) copy-start(f32[1,2,2,128,128]{4,3,2,1,0:T(8,128)} %param.16) | copy-start | bytes 786436
  49.8 108.7 %all-to-all-start = ((bf16[2,32,1,128,512]{4,3,0,2,1:T(8,128)(2,1)}), bf16[2,32,1,128,512]{4,3,0,2,1:T(8,128)(2,1)}, u32[]{:S(2)}, u32[]{:S(2)}) async-start(bf16[2,32,1,128,512]{4,3,0,2,1:T(8,128)(2,1)} %copy.78), calls=%async_computation | async-start | bytes 16777216 | tf_op jit(solution)/shard_map/all_to_all | solution.py:71
  158.4 16.9 %all-to-all-start.1 = ((s32[1,32,1,128]{3,2,0,1:T(1,128)}), s32[1,32,1,128]{3,2,0,1:T(1,128)S(1)}, u32[]{:S(2)}, u32[]{:S(2)}) async-start(s32[1,32,1,128]{3,2,0,1:T(1,128)} %bitcast.32), calls=%async_computation.1 | async-start | bytes 32768 | tf_op jit(solution)/shard_map/all_to_all | solution.py:72
  182.1 3.5 copy-start.13
  185.6 27.9 %collective-permute-start = (f32[2,256,512]{2,1,0:T(8,128)}, f32[2,256,512]{2,1,0:T(8,128)}, u32[]{:S(2)}, u32[]{:S(2)}) collective-permute-start(f32[2,256,512]{2,1,0:T(8,128)} %get-tuple-element.88), channel_id=1, source_target_pairs={{0,32},{32,64},{64,96},{96,128},{128,160},{160,192},{192,224},{1,3... | collective-permute-start | bytes 3145736 | tf_op jit(solution)/shard_map/while/body/eval_jaxpr/ppermute | solution.py:10
  218.4 27.0 %collective-permute-start = (f32[2,256,512]{2,1,0:T(8,128)}, f32[2,256,512]{2,1,0:T(8,128)}, u32[]{:S(2)}, u32[]{:S(2)}) collective-permute-start(f32[2,256,512]{2,1,0:T(8,128)} %get-tuple-element.88), channel_id=1, source_target_pairs={{0,32},{32,64},{64,96},{96,128},{128,160},{160,192},{192,224},{1,3... | collective-permute-start | bytes 3145736 | tf_op jit(solution)/shard_map/while/body/eval_jaxpr/ppermute | solution.py:10
  250.4 26.2 %collective-permute-start = (f32[2,256,512]{2,1,0:T(8,128)}, f32[2,256,512]{2,1,0:T(8,128)}, u32[]{:S(2)}, u32[]{:S(2)}) collective-permute-start(f32[2,256,512]{2,1,0:T(8,128)} %get-tuple-element.88), channel_id=1, source_target_pairs={{0,32},{32,64},{64,96},{96,128},{128,160},{160,192},{192,224},{1,3... | collective-permute-start | bytes 3145736 | tf_op jit(solution)/shard_map/while/body/eval_jaxpr/ppermute | solution.py:10
  281.6 25.3 %collective-permute-start = (f32[2,256,512]{2,1,0:T(8,128)}, f32[2,256,512]{2,1,0:T(8,128)}, u32[]{:S(2)}, u32[]{:S(2)}) collective-permute-start(f32[2,256,512]{2,1,0:T(8,128)} %get-tuple-element.88), channel_id=1, source_target_pairs={{0,32},{32,64},{64,96},{96,128},{128,160},{160,192},{192,224},{1,3... | collective-permute-start | bytes 3145736 | tf_op jit(solution)/shard_map/while/body/eval_jaxpr/ppermute | solution.py:10
  311.9 24.5 %collective-permute-start = (f32[2,256,512]{2,1,0:T(8,128)}, f32[2,256,512]{2,1,0:T(8,128)}, u32[]{:S(2)}, u32[]{:S(2)}) collective-permute-start(f32[2,256,512]{2,1,0:T(8,128)} %get-tuple-element.88), channel_id=1, source_target_pairs={{0,32},{32,64},{64,96},{96,128},{128,160},{160,192},{192,224},{1,3... | collective-permute-start | bytes 3145736 | tf_op jit(solution)/shard_map/while/body/eval_jaxpr/ppermute | solution.py:10
  341.3 23.6 %collective-permute-start = (f32[2,256,512]{2,1,0:T(8,128)}, f32[2,256,512]{2,1,0:T(8,128)}, u32[]{:S(2)}, u32[]{:S(2)}) collective-permute-start(f32[2,256,512]{2,1,0:T(8,128)} %get-tuple-element.88), channel_id=1, source_target_pairs={{0,32},{32,64},{64,96},{96,128},{128,160},{160,192},{192,224},{1,3... | collective-permute-start | bytes 3145736 | tf_op jit(solution)/shard_map/while/body/eval_jaxpr/ppermute | solution.py:10
  369.9 22.8 %collective-permute-start = (f32[2,256,512]{2,1,0:T(8,128)}, f32[2,256,512]{2,1,0:T(8,128)}, u32[]{:S(2)}, u32[]{:S(2)}) collective-permute-start(f32[2,256,512]{2,1,0:T(8,128)} %get-tuple-element.88), channel_id=1, source_target_pairs={{0,32},{32,64},{64,96},{96,128},{128,160},{160,192},{192,224},{1,3... | collective-permute-start | bytes 3145736 | tf_op jit(solution)/shard_map/while/body/eval_jaxpr/ppermute | solution.py:10
  544.2 9.2 %copy-start.3 = (bf16[1,16,2,128,128]{4,3,1,2,0:T(8,128)(2,1)S(1)}, bf16[1,16,2,128,128]{4,3,1,2,0:T(8,128)(2,1)}, u32[]{:S(2)}) copy-start(bf16[1,16,2,128,128]{4,3,1,2,0:T(8,128)(2,1)} %copy-done.2) | copy-start | bytes 3145732
  553.3 2.4 copy-start.7
  556.5 1.6 copy-start.6
  558.1 1.2 copy-start.5
  561.5 1.6 copy-start.1
where the time goes:
time: 573 us; the launch traced here: 566 us
  waiting for transfers between devices  263 us (46%)
  blocking collectives  108 us (19%)
  matrix products  69.3 us (12%)
  local copies, waits for them, and re-layouts  68.5 us (12%)
  starting transfers between devices  31.3 us (5%)
  other arithmetic  24.5 us (4%)
    ppermute x7, waiting for transfers between devices, passed_along(): return lax.ppermute(x, axis, pairs)  163 us
    all_to_all x1, blocking collectives, body(): lax.all_to_all(slot_rows, 'front', split_axis=1, concat_axis=1, tiled=True)  108 us
    all_to_all x1, waiting for transfers between devices, body(): lax.all_to_all(placed, 'front', split_axis=1, concat_axis=1, tiled=True)  99.9 us
    unnamed x36, local copies, waits for them, and re-layouts  15 us
    ppermute x7, starting transfers between devices, passed_along(): return lax.ppermute(x, axis, pairs)  14.1 us
    reshape x1, local copies, waits for them, and re-layouts, body(): slot_rows = slot_rows.reshape(2, fronts, per_owner, blk, width)  14 us
  transfers between devices with their start and end apart: 9, of which 8 were waited for; matrix products, arithmetic and copies ran while one was open for 1% of the time, Pallas kernels for 0%

commit v1 on v0

--- a/solution.py
+++ b/solution.py
@@ -68,7 +68,12 @@
     ).astype(jnp.bfloat16)
     placed = placed.reshape(2, fronts, per_owner, blk, width)
     arrived, arrived_ids = (
-        lax.all_to_all(placed, "front", split_axis=1, concat_axis=1, tiled=True),
+        jnp.concatenate(
+            lax.all_to_all(
+                jnp.stack(jnp.split(placed, lax.axis_size("front"), axis=1)), "front", 0, 0
+            ),
+            axis=1,
+        ),
         lax.all_to_all(slot_ids, "front", split_axis=1, concat_axis=1, tiled=True),
     )
     slot_parts = arrived.reshape(2, slot_total * blk, width)

time: 573 us -> 633 us (1.10)
  local copies, waits for them, and re-layouts: 68.5 us -> 120 us
  matrix products: 69.3 us -> 77.1 us
    unnamed x36 -> x67, local copies, waits for them, and re-layouts: 15 us -> 37.7 us
    split x0 -> x2, local copies, waits for them, and re-layouts: none -> 17.1 us  [body(): jnp.split(placed, lax.axis_size('front'), axis=1)]
    all_to_all x1, local copies, waits for them, and re-layouts: 7.62 us -> 14.7 us  [body(): lax.all_to_all(slot_rows, 'front', split_axis=1, concat_axis=1, tiled=True)]
where the time goes in v1:
time: 633 us; the launch traced here: 627 us
  waiting for transfers between devices  263 us (42%)
  local copies, waits for them, and re-layouts  120 us (19%)
  blocking collectives  108 us (17%)
  matrix products  77.1 us (12%)
  starting transfers between devices  31.3 us (5%)
  other arithmetic  25.2 us (4%)
    ppermute x7, waiting for transfers between devices, passed_along(): return lax.ppermute(x, axis, pairs)  163 us
    all_to_all x1, blocking collectives, body(): lax.all_to_all(slot_rows, 'front', split_axis=1, concat_axis=1, tiled=True)  108 us
    all_to_all x1, waiting for transfers between devices, body(): lax.all_to_all(jnp.stack(jnp.split(placed, lax.axis_size('front'), axis=1...  99.9 us
    unnamed x67, local copies, waits for them, and re-layouts  37.7 us
    split x2, local copies, waits for them, and re-layouts, body(): jnp.split(placed, lax.axis_size('front'), axis=1)  17.1 us
    all_to_all x1, local copies, waits for them, and re-layouts, body(): lax.all_to_all(slot_rows, 'front', split_axis=1, concat_axis=1, tiled=True)  14.7 us
    ppermute x7, starting transfers between devices, passed_along(): return lax.ppermute(x, axis, pairs)  14.1 us
  transfers between devices with their start and end apart: 9, of which 8 were waited for; matrix products, arithmetic and copies ran while one was open for 1% of the time, Pallas kernels for 0%

profile of v1, /device:TPU:129, one launch (start us, length us, event | category | flops | bytes accessed | tf_op | source)
XLA Modules:
  0.0 626.8 jit_solution(15159104053771282709)
XLA Ops:
  13.5 5.1 copy.1171
  18.6 4.4 fusion.35
  23.0 4.5 copy.1172
  27.8 4.7 convert_bitcast_fusion
  32.4 7.1 %fusion.61 = (bf16[2,1,1,128,512]{4,1,3,0,2:T(2,128)(2,1)S(1)}, bf16[2,1,1,128,512]{4,1,3,0,2:T(2,128)(2,1)S(1)}, bf16[2,1,1,128,512]{4,1,3,0,2:T(2,128)(2,1)S(1...) fusion(bf16[2,32,1,128,512]{4,1,3,0,2:T(8,128)(2,1)S(1)} %conve, ...), kind=kLoop, calls=%fused_computation.119 | loop fusion | bytes 6815744 | tf_op jit(solution)/shard_map/split | solution.py:73
  39.5 10.1 %fusion.60 = (bf16[2,1,1,128,512]{4,1,3,0,2:T(2,128)(2,1)S(1)}, bf16[2,1,1,128,512]{4,1,3,0,2:T(2,128)(2,1)S(1)}, bf16[2,1,1,128,512]{4,1,3,0,2:T(2,128)(2,1)S(1...) fusion(bf16[2,32,1,128,512]{4,1,3,0,2:T(8,128)(2,1)S(1)} %conve, ...), kind=kLoop, calls=%fused_computation.118 | loop fusion | bytes 9961472 | tf_op jit(solution)/shard_map/split | solution.py:73
  73.4 8.0 %all-to-all-start = ((bf16[32,2,1,1,128,512]{5,4,1,3,2,0:T(8,128)(2,1)}), bf16[32,2,1,1,128,512]{5,4,1,3,2,0:T(8,128)(2,1)}, u32[]{:S(2)}, u32[]{:S(2)}) async-start(bf16[32,2,1,1,128,512]{5,4,1,3,2,0:T(8,128)(2,1)} %bitcast_dynamic-update-slice_fusion), calls=%async_computation | async-start | bytes 16777216 | tf_op jit(solution)/shard_map/all_to_all | solution.py:72
  82.2 99.9 %all-to-all-done = bf16[32,2,1,1,128,512]{5,4,1,3,2,0:T(8,128)(2,1)} async-done(((bf16[32,2,1,1,128,512]{5,4,1,3,2,0:T(8,128)(2,1)}), bf16[32,2,1,1,128,512]{5,4,1,3,2,0:T(8,128)(2,1)}, u32[]{:S(2)}, u32[]{:S(2)}) %all-to-all-start) | async-done | bytes 8388640 | tf_op jit(solution)/shard_map/all_to_all | solution.py:72
  182.1 9.2 %all-to-all-start.1 = ((s32[1,32,1,128]{3,2,0,1:T(1,128)}), s32[1,32,1,128]{3,2,0,1:T(1,128)S(1)}, u32[]{:S(2)}, u32[]{:S(2)}) async-start(s32[1,32,1,128]{3,2,0,1:T(1,128)} %bitcast.34), calls=%async_computation.1 | async-start | bytes 32768 | tf_op jit(solution)/shard_map/all_to_all | solution.py:77
  191.4 7.6 %copy.1173 = bf16[2,32,1,1,128,512]{5,4,1,0,3,2:T(8,128)(2,1)} copy(bf16[2,32,1,1,128,512]{5,4,0,3,2,1:T(8,128)(2,1)} %bitcast.30) | data formatting | bytes 16777216 | tf_op jit(solution)/shard_map/reshape | solution.py:71
  199.0 6.7 %fusion.39 = f32[2,256,512]{2,1,0:T(8,128)S(1)} fusion(bf16[2,4096,512]{2,1,0:T(8,128)(2,1)} %bitcast.293, s32[4096]{0:T(1024)S(1)} %bitcast.301, bf16[1,2,256,512]{3,2,1,0:T(8,128)(2,1)} %param.15), kind=kOutput, calls=%fused_computation.52 | convolution fusion | flops 2149056512 | bytes 9977856 | tf_op jit(solution)/shard_map/sr,psc->prc/dot_general | solution.py:84
  209.2 212.0 %while.10 = (s32[]{:T(128)}, f32[2,256,512]{2,1,0:T(8,128)}, f32[1,256]{1,0:T(1,128)S(1)}, f32[2,256,512]{2,1,0:T(8,128)S(1)}, f32[2,2,128,128]{3,2,0,1:T(8,128)S(1)}, /*index=5*/s32[]{:T(128)}) while((s32[]{:T(128)}, f32[2,256,512]{2,1,0:T(8,128)}, f32[1,256]{1,0:T(1,128)S(1)}, f32[2,256,512]{2,1,0:T(8,128)S(1)}, ...), condition=%wide.region_4.5_spmd, body=%wide.region_3.4_spmd.sunk | while | flops 806354944 | bytes 17302636 | solution.py:94
  211.9 25.3 %collective-permute-done = f32[2,256,512]{2,1,0:T(8,128)} collective-permute-done((f32[2,256,512]{2,1,0:T(8,128)}, f32[2,256,512]{2,1,0:T(8,128)}, u32[]{:S(2)}, u32[]{:S(2)}) %collective-permute-start) | collective-permute-done | bytes 1048608 | tf_op jit(solution)/shard_map/while/body/eval_jaxpr/ppermute | solution.py:10
  244.0 25.1 %collective-permute-done = f32[2,256,512]{2,1,0:T(8,128)} collective-permute-done((f32[2,256,512]{2,1,0:T(8,128)}, f32[2,256,512]{2,1,0:T(8,128)}, u32[]{:S(2)}, u32[]{:S(2)}) %collective-permute-start) | collective-permute-done | bytes 1048608 | tf_op jit(solution)/shard_map/while/body/eval_jaxpr/ppermute | solution.py:10
  276.0 24.3 %collective-permute-done = f32[2,256,512]{2,1,0:T(8,128)} collective-permute-done((f32[2,256,512]{2,1,0:T(8,128)}, f32[2,256,512]{2,1,0:T(8,128)}, u32[]{:S(2)}, u32[]{:S(2)}) %collective-permute-start) | collective-permute-done | bytes 1048608 | tf_op jit(solution)/shard_map/while/body/eval_jaxpr/ppermute | solution.py:10
  307.1 23.4 %collective-permute-done = f32[2,256,512]{2,1,0:T(8,128)} collective-permute-done((f32[2,256,512]{2,1,0:T(8,128)}, f32[2,256,512]{2,1,0:T(8,128)}, u32[]{:S(2)}, u32[]{:S(2)}) %collective-permute-start) | collective-permute-done | bytes 1048608 | tf_op jit(solution)/shard_map/while/body/eval_jaxpr/ppermute | solution.py:10
  337.4 22.6 %collective-permute-done = f32[2,256,512]{2,1,0:T(8,128)} collective-permute-done((f32[2,256,512]{2,1,0:T(8,128)}, f32[2,256,512]{2,1,0:T(8,128)}, u32[]{:S(2)}, u32[]{:S(2)}) %collective-permute-start) | collective-permute-done | bytes 1048608 | tf_op jit(solution)/shard_map/while/body/eval_jaxpr/ppermute | solution.py:10
  366.9 21.7 %collective-permute-done = f32[2,256,512]{2,1,0:T(8,128)} collective-permute-done((f32[2,256,512]{2,1,0:T(8,128)}, f32[2,256,512]{2,1,0:T(8,128)}, u32[]{:S(2)}, u32[]{:S(2)}) %collective-permute-start) | collective-permute-done | bytes 1048608 | tf_op jit(solution)/shard_map/while/body/eval_jaxpr/ppermute | solution.py:10
  395.4 20.8 %collective-permute-done = f32[2,256,512]{2,1,0:T(8,128)} collective-permute-done((f32[2,256,512]{2,1,0:T(8,128)}, f32[2,256,512]{2,1,0:T(8,128)}, u32[]{:S(2)}, u32[]{:S(2)}) %collective-permute-start) | collective-permute-done | bytes 1048608 | tf_op jit(solution)/shard_map/while/body/eval_jaxpr/ppermute | solution.py:10
  421.2 6.8 %convolution_convert_fusion = bf16[2,512,4096]{2,1,0:T(8,128)(2,1)} fusion(s32[4096]{0:T(1024)S(1)} %bitcast.302, f32[2,256,512]{2,1,0:T(8,128)} %get-tuple-element.29), kind=kOutput, calls=%fused_computation.19 | convolution fusion | flops 2152988672 | bytes 9453568 | tf_op jit(solution)/shard_map/sr,prc->psc/dot_general | solution.py:96
  428.1 9.5 %copy.1226 = bf16[128,8,32,128]{3,2,1,0:T(8,128)(2,1)} copy(bf16[128,8,32,128]{3,1,2,0:T(8,128)(2,1)} %bitcast.271) | data formatting | bytes 16777216
  437.6 9.9 %copy.1178 = bf16[2,32,1,128,512]{3,4,0,2,1:T(8,128)(2,1)} copy(bf16[2,32,1,128,512]{3,1,4,0,2:T(8,128)(2,1)} %bitcast.272) | data formatting | bytes 16777216 | tf_op jit(solution)/shard_map/reshape | solution.py:99
  447.4 108.2 %all_to_all.15 = bf16[2,32,1,128,512]{3,4,0,2,1:T(8,128)(2,1)} all-to-all(bf16[2,32,1,128,512]{3,4,0,2,1:T(8,128)(2,1)} %copy.1178), channel_id=1, replica_groups=mesh['slab'=8,'front'=32] {'front'}, dimensions={1} | all-to-all | bytes 16777216 | tf_op jit(solution)/shard_map/all_to_all | solution.py:100
  555.6 14.7 %copy.1179 = bf16[2,32,1,128,512]{4,1,3,0,2:T(8,128)(2,1)} copy(bf16[2,32,1,128,512]{3,4,0,2,1:T(8,128)(2,1)} %all_to_all.15) | data formatting | bytes 16777216 | tf_op jit(solution)/shard_map/all_to_all | solution.py:100
  570.3 4.7 convert_bitcast_fusion.1
  577.4 4.7 copy.1180
  582.1 4.3 fusion.46
  586.4 4.6 copy.1181
  604.1 5.5 copy.1184
  609.6 5.5 add_bitcast_fusion
  615.1 5.4 copy.1185
  620.5 6.0 fusion.10
  (150 shorter events, 105.3 us)
Async XLA Ops:
  0.6 4.2 copy-start.9
  2.1 4.8 copy-start.3
  5.6 1.2 copy-start.11
  6.9 11.7 %copy-start.1 = (bf16[1,16,2,128,128]{4,3,1,2,0:T(8,128)(2,1)}, bf16[1,16,2,128,128]{4,3,1,2,0:T(8,128)(2,1)S(1)}, u32[]{:S(2)}) copy-start(bf16[1,16,2,128,128]{4,3,1,2,0:T(8,128)(2,1)S(1)} %copy.1262) | copy-start | bytes 3145732
  7.6 3.6 copy-start
  23.0 4.5 copy-start.15
  73.4 8.1 %copy-start.14 = (s32[1,16,128]{2,1,0:T(8,128)S(1)}, s32[1,16,128]{2,1,0:T(8,128)}, u32[]{:S(2)}) copy-start(s32[1,16,128]{2,1,0:T(8,128)} %param.14) | copy-start | bytes 24580
  73.4 117.9 %copy-start.12 = (f32[1,2,2,128,128]{4,3,2,1,0:T(8,128)S(1)}, f32[1,2,2,128,128]{4,3,2,1,0:T(8,128)}, u32[]{:S(2)}) copy-start(f32[1,2,2,128,128]{4,3,2,1,0:T(8,128)} %param.16) | copy-start | bytes 786436
  73.4 108.7 %all-to-all-start = ((bf16[32,2,1,1,128,512]{5,4,1,3,2,0:T(8,128)(2,1)}), bf16[32,2,1,1,128,512]{5,4,1,3,2,0:T(8,128)(2,1)}, u32[]{:S(2)}, u32[]{:S(2)}) async-start(bf16[32,2,1,1,128,512]{5,4,1,3,2,0:T(8,128)(2,1)} %bitcast_dynamic-update-slice_fusion), calls=%async_computation | async-start | bytes 16777216 | tf_op jit(solution)/shard_map/all_to_all | solution.py:72
  182.1 16.9 %all-to-all-start.1 = ((s32[1,32,1,128]{3,2,0,1:T(1,128)}), s32[1,32,1,128]{3,2,0,1:T(1,128)S(1)}, u32[]{:S(2)}, u32[]{:S(2)}) async-start(s32[1,32,1,128]{3,2,0,1:T(1,128)} %bitcast.34), calls=%async_computation.1 | async-start | bytes 32768 | tf_op jit(solution)/shard_map/all_to_all | solution.py:77
  205.7 3.5 copy-start.13
  209.2 27.9 %collective-permute-start = (f32[2,256,512]{2,1,0:T(8,128)}, f32[2,256,512]{2,1,0:T(8,128)}, u32[]{:S(2)}, u32[]{:S(2)}) collective-permute-start(f32[2,256,512]{2,1,0:T(8,128)} %get-tuple-element.120), channel_id=1, source_target_pairs={{0,32},{32,64},{64,96},{96,128},{128,160},{160,192},{192,224},{1,3... | collective-permute-start | bytes 3145736 | tf_op jit(solution)/shard_map/while/body/eval_jaxpr/ppermute | solution.py:10
  242.1 27.0 %collective-permute-start = (f32[2,256,512]{2,1,0:T(8,128)}, f32[2,256,512]{2,1,0:T(8,128)}, u32[]{:S(2)}, u32[]{:S(2)}) collective-permute-start(f32[2,256,512]{2,1,0:T(8,128)} %get-tuple-element.120), channel_id=1, source_target_pairs={{0,32},{32,64},{64,96},{96,128},{128,160},{160,192},{192,224},{1,3... | collective-permute-start | bytes 3145736 | tf_op jit(solution)/shard_map/while/body/eval_jaxpr/ppermute | solution.py:10
  274.1 26.2 %collective-permute-start = (f32[2,256,512]{2,1,0:T(8,128)}, f32[2,256,512]{2,1,0:T(8,128)}, u32[]{:S(2)}, u32[]{:S(2)}) collective-permute-start(f32[2,256,512]{2,1,0:T(8,128)} %get-tuple-element.120), channel_id=1, source_target_pairs={{0,32},{32,64},{64,96},{96,128},{128,160},{160,192},{192,224},{1,3... | collective-permute-start | bytes 3145736 | tf_op jit(solution)/shard_map/while/body/eval_jaxpr/ppermute | solution.py:10
  305.2 25.3 %collective-permute-start = (f32[2,256,512]{2,1,0:T(8,128)}, f32[2,256,512]{2,1,0:T(8,128)}, u32[]{:S(2)}, u32[]{:S(2)}) collective-permute-start(f32[2,256,512]{2,1,0:T(8,128)} %get-tuple-element.120), channel_id=1, source_target_pairs={{0,32},{32,64},{64,96},{96,128},{128,160},{160,192},{192,224},{1,3... | collective-permute-start | bytes 3145736 | tf_op jit(solution)/shard_map/while/body/eval_jaxpr/ppermute | solution.py:10
  335.5 24.5 %collective-permute-start = (f32[2,256,512]{2,1,0:T(8,128)}, f32[2,256,512]{2,1,0:T(8,128)}, u32[]{:S(2)}, u32[]{:S(2)}) collective-permute-start(f32[2,256,512]{2,1,0:T(8,128)} %get-tuple-element.120), channel_id=1, source_target_pairs={{0,32},{32,64},{64,96},{96,128},{128,160},{160,192},{192,224},{1,3... | collective-permute-start | bytes 3145736 | tf_op jit(solution)/shard_map/while/body/eval_jaxpr/ppermute | solution.py:10
  364.9 23.6 %collective-permute-start = (f32[2,256,512]{2,1,0:T(8,128)}, f32[2,256,512]{2,1,0:T(8,128)}, u32[]{:S(2)}, u32[]{:S(2)}) collective-permute-start(f32[2,256,512]{2,1,0:T(8,128)} %get-tuple-element.120), channel_id=1, source_target_pairs={{0,32},{32,64},{64,96},{96,128},{128,160},{160,192},{192,224},{1,3... | collective-permute-start | bytes 3145736 | tf_op jit(solution)/shard_map/while/body/eval_jaxpr/ppermute | solution.py:10
  393.5 22.8 %collective-permute-start = (f32[2,256,512]{2,1,0:T(8,128)}, f32[2,256,512]{2,1,0:T(8,128)}, u32[]{:S(2)}, u32[]{:S(2)}) collective-permute-start(f32[2,256,512]{2,1,0:T(8,128)} %get-tuple-element.120), channel_id=1, source_target_pairs={{0,32},{32,64},{64,96},{96,128},{128,160},{160,192},{192,224},{1,3... | collective-permute-start | bytes 3145736 | tf_op jit(solution)/shard_map/while/body/eval_jaxpr/ppermute | solution.py:10
  577.4 4.7 copy-start.2
  591.0 2.4 copy-start.7
  591.0 3.5 copy-start.10
  594.4 1.2 copy-start.4
  595.6 3.1 copy-start.8
  595.6 2.3 copy-start.6
  604.1 5.5 copy-start.5
